TPU v7x, 32 devices: a whole 2x2x4 slice. The times are simulated.
32 devices in a mesh: groups: 2 (over x), wide: 16 (over z, y, core).
Axes of the slice: x: 2, y: 2, z: 4, core: 2. Of those that a mesh axis runs over, the one named last changes fastest.
Arguments:
- voltages: bfloat16 [512, 265216], P('wide', 'groups'), parts along dimension 1, may hold values from -6 to 6
- antenna_flags: int32 [1024], P(('groups', 'wide')), parts along dimension 0, may hold values 0 or 1
- baseline_pairs: int32 [2, 2048], replicated, may hold values from 0 to 511, as said below
Outputs:
- delay_power: float32 [512, 2048], P('groups', 'wide'), parts along dimension 0
There are 2 independent parts, one for each index of `groups`. A program takes and returns all parts, laid end to end along the dimension named above; an argument that names none is the same for every part. Nothing has to cross between parts.
Inputs may be any that keep to these rules, and one draw needn't show every extreme that they name: `baseline_pairs`: the two inputs of a baseline always differ; baseline 0 pairs input 0 with input 512 - 1.
All inputs are finite; a program needn't handle non-finite values. No bound on the sum of `antenna_flags` on one device may be relied on, other than what follows from the above.
Results may differ from a plain program's by a relative error of at most 0.0055.
Values may be sent and summed in bfloat16 or wider, within the bound.
No kernel may reach another device: no remote copies, remote signals or barrier semaphores. Data moves between devices by JAX's collectives and lax.ppermute only.
A program may use at most 192 MiB of HBM per device.

v0:
```python
import math

import jax
import jax.numpy as jnp
import numpy as np
from jax import lax
from jax.experimental import pallas as pl
from jax.experimental.pallas import tpu as pltpu
from jax.sharding import PartitionSpec as P

INPUT_COUNT = 512
CHANNEL_COUNT = 256
TAPS = 4
NT = 128
NFFT = 512
HALF = NFFT // 2
FRAMES = 2 * NT

CHUNKS = (96, 128, 32)
BANK_STEP = 8
CORR_STEP = 32
LANES = 128
BASE_TILE = 256


def prototype_np():
    count = TAPS * NFFT
    m = np.arange(count, dtype=np.float64)
    shift = (m - count / 2 + 0.5) / NFFT
    hamming = 0.54 - 0.46 * np.cos(2 * np.pi * m / (count - 1))
    return (np.sinc(shift) * hamming).reshape(TAPS, NFFT).astype(np.float32)


def transform_np(parity, width):
    local = CHANNEL_COUNT // width
    owner = np.arange(width)[:, None, None]
    m = np.arange(local // 2)[None, None, :]
    channel = np.broadcast_to(owner * local + 2 * m + parity, (width, 2, local // 2))
    is_real = np.broadcast_to(np.arange(2)[None, :, None] == 0, channel.shape)
    phase = channel.reshape(-1, 1) * np.arange(HALF)[None, :] % NFFT
    angle = 2 * np.pi * phase / NFFT
    table = np.where(is_real.reshape(-1, 1), np.cos(angle), -np.sin(angle)) / math.sqrt(NFFT)
    high = table.astype(jnp.bfloat16)
    low = (table - high.astype(np.float64)).astype(jnp.bfloat16)
    return np.concatenate([high, high, low], axis=1)


def delay_np(width):
    chan = np.arange(CHANNEL_COUNT)
    base = 2 * np.pi * chan / (CHANNEL_COUNT - 1)
    window = 0.35875 - 0.48829 * np.cos(base) + 0.14128 * np.cos(2 * base) - 0.01168 * np.cos(3 * base)
    angle = 2 * np.pi * (chan[:, None] * chan[None, :] % CHANNEL_COUNT) / CHANNEL_COUNT
    cosine = np.cos(angle) * window[None, :]
    sine = np.sin(angle) * window[None, :]
    upper = np.stack([cosine, sine])
    lower = np.stack([-sine, cosine])
    table = np.concatenate([upper, lower], axis=1) / math.sqrt(np.sum(window * window))
    local = CHANNEL_COUNT // width
    table = table.reshape(2, 2 * CHANNEL_COUNT, width, local // 2, 2).transpose(1, 2, 4, 0, 3)
    return table.reshape(2 * CHANNEL_COUNT, 2 * CHANNEL_COUNT).astype(np.float32).astype(jnp.bfloat16)


def bank_kernel(x_ref, h0_ref, h1_ref, h2_ref, proto_ref, flag_ref, even_ref, odd_ref, y_ref, e_ref, o_ref):
    inputs = x_ref.shape[0]
    rows = 16
    halo = (h0_ref, h1_ref, h2_ref)

    def frame(t, at, column):
        if t < BANK_STEP:
            return x_ref[at : at + rows, t * NFFT + column : t * NFFT + column + LANES].astype(jnp.float32)
        return halo[t - BANK_STEP][at : at + rows, column : column + LANES].astype(jnp.float32)

    for at in range(0, inputs, rows):
        flag = flag_ref[at : at + rows, :]
        for column in range(0, HALF, LANES):
            parts = []
            for side in (column, column + HALF):
                taps = [proto_ref[tap : tap + 1, side : side + LANES] for tap in range(TAPS)]
                window = [frame(t, at, side) for t in range(TAPS - 1)]
                sums = []
                for t in range(BANK_STEP):
                    window.append(frame(t + TAPS - 1, at, side))
                    total = taps[0] * window[0]
                    for tap in range(1, TAPS):
                        total = total + taps[tap] * window[tap]
                    sums.append(total * flag)
                    window.pop(0)
                parts.append(sums)
            for t in range(BANK_STEP):
                first, second = parts[0][t], parts[1][t]
                at_rows = slice(t * inputs + at, t * inputs + at + rows)
                for ref, value in ((e_ref, first + second), (o_ref, first - second)):
                    high = value.astype(jnp.bfloat16)
                    low = (value - high.astype(jnp.float32)).astype(jnp.bfloat16)
                    ref[at_rows, column : column + LANES] = high
                    ref[at_rows, HALF + column : HALF + column + LANES] = low
                    ref[at_rows, 2 * HALF + column : 2 * HALF + column + LANES] = high
    contract = (((1,), (1,)), ((), ()))
    width = y_ref.shape[0]
    part = y_ref.shape[1] // 2
    for parity, (table, data) in enumerate(((even_ref, e_ref), (odd_ref, o_ref))):
        out = lax.dot_general(table[...], data[...], contract, preferred_element_type=jnp.float32)
        out = out.astype(jnp.bfloat16).reshape(width, part, out.shape[1])
        y_ref[:, parity * part : (parity + 1) * part, :] = out


def filter_bank(voltages, proto, flags, even, odd, first, count, width):
    inputs = voltages.shape[0]
    local = CHANNEL_COUNT // width
    step_lanes = BANK_STEP * inputs
    main = pl.BlockSpec((inputs, BANK_STEP * NFFT), lambda j: (0, first // BANK_STEP + j))
    halos = [
        pl.BlockSpec((inputs, NFFT), lambda j, h=h: (0, first + (j + 1) * BANK_STEP + h)) for h in range(TAPS - 1)
    ]
    whole = lambda a: pl.BlockSpec(a.shape, lambda j: (0, 0))
    return pl.pallas_call(
        bank_kernel,
        grid=(count // BANK_STEP,),
        in_specs=[main, *halos, whole(proto), whole(flags), whole(even), whole(odd)],
        out_specs=pl.BlockSpec((width, 2 * local, step_lanes), lambda j: (0, 0, j)),
        out_shape=jax.ShapeDtypeStruct((width, 2 * local, count * inputs), jnp.bfloat16),
        scratch_shapes=[pltpu.VMEM((step_lanes, 3 * HALF), jnp.bfloat16)] * 2,
        compiler_params=pltpu.CompilerParams(vmem_limit_bytes=32 * 2**20),
        cost_estimate=pl.CostEstimate(
            flops=2 * 3 * count * inputs * NFFT * HALF, bytes_accessed=4 * count * inputs * NFFT, transcendentals=0
        ),
        name="bank",
    )(voltages, voltages, voltages, voltages, proto, flags, even, odd)


def corr_kernel(z_ref, first_ref, second_ref, past_ref, out_ref, rows_ref):
    sources, planes, lanes = z_ref.shape
    inputs = INPUT_COUNT // sources
    group = LANES // inputs
    half = planes // 2
    eighth = planes // 4
    frames = lanes // inputs
    step = pl.program_id(0)

    @pl.when(step == 0)
    def _():
        out_ref[...] = past_ref[...]

    for block in range(lanes // LANES):
        for lead in range(0, sources, group):
            tiles = [z_ref[lead + s, :, block * LANES : (block + 1) * LANES] for s in range(group)]
            for t in range(group):
                joined = jnp.concatenate([tile[:, t * inputs : (t + 1) * inputs] for tile in tiles], axis=1)
                at = (block * group + t) * planes
                rows_ref[at : at + planes, lead * inputs : lead * inputs + LANES] = joined

    def tile(k, carry):
        at = pl.ds(pl.multiple_of(k * BASE_TILE, BASE_TILE), BASE_TILE)
        first = jnp.dot(rows_ref[...], first_ref[:, at], preferred_element_type=jnp.float32)
        second = jnp.dot(rows_ref[...], second_ref[:, at], preferred_element_type=jnp.float32)
        first = first.reshape(frames, 2, 2, eighth, BASE_TILE)
        second = second.reshape(frames, 2, 2, eighth, BASE_TILE)
        real = jnp.sum(first[:, :, 0] * second[:, :, 0] + first[:, :, 1] * second[:, :, 1], axis=0)
        imag = jnp.sum(first[:, :, 1] * second[:, :, 0] - first[:, :, 0] * second[:, :, 1], axis=0)
        for parity in range(2):
            base = parity * half
            out_ref[base : base + eighth, at] += real[parity]
            out_ref[base + eighth : base + half, at] += imag[parity]
        return carry

    lax.fori_loop(0, first_ref.shape[1] // BASE_TILE, tile, 0)


def correlate(received, first, second, past):
    sources, planes, lanes = received.shape
    inputs = INPUT_COUNT // sources
    step_lanes = CORR_STEP * inputs
    count = first.shape[1]
    whole = lambda a: pl.BlockSpec(a.shape, lambda j: (0, 0))
    return pl.pallas_call(
        corr_kernel,
        grid=(lanes // step_lanes,),
        in_specs=[
            pl.BlockSpec((sources, planes, step_lanes), lambda j: (0, 0, j)),
            whole(first),
            whole(second),
            whole(past),
        ],
        out_specs=pl.BlockSpec((planes, count), lambda j: (0, 0)),
        out_shape=jax.ShapeDtypeStruct((planes, count), jnp.float32),
        scratch_shapes=[pltpu.VMEM((CORR_STEP * planes, INPUT_COUNT), jnp.bfloat16)],
        compiler_params=pltpu.CompilerParams(vmem_limit_bytes=48 * 2**20),
        cost_estimate=pl.CostEstimate(
            flops=4 * (lanes // inputs) * planes * INPUT_COUNT * count,
            bytes_accessed=2 * sources * planes * lanes + 4 * INPUT_COUNT * count,
            transcendentals=0,
        ),
        name="corr",
    )(received, first, second, past)


def power_kernel(table_ref, values_ref, out_ref):
    delays = jnp.dot(table_ref[...], values_ref[...], preferred_element_type=jnp.float32)
    out_ref[...] = delays[:CHANNEL_COUNT] ** 2 + delays[CHANNEL_COUNT:] ** 2


def delay_power(table, values):
    return pl.pallas_call(
        power_kernel,
        out_shape=jax.ShapeDtypeStruct((CHANNEL_COUNT, values.shape[1]), jnp.float32),
        name="power",
    )(table, values)


def prototype_table():
    count = TAPS * NFFT
    positions = jnp.arange(count, dtype=jnp.float32)
    start_shift = (positions - count / 2 + 0.5) / NFFT
    hamming = 0.54 - 0.46 * jnp.cos(2 * jnp.pi * positions / (count - 1))
    return (jnp.sinc(start_shift) * hamming).reshape(TAPS, NFFT)


def plain_filter_bank(voltages, antenna_flags, first_input, count):
    framed = voltages.astype(jnp.float32).reshape(voltages.shape[0], -1, NFFT)
    prototype = prototype_table()
    filtered = jnp.zeros((voltages.shape[0], count, NFFT), jnp.float32)
    for tap_index in range(TAPS):
        filtered = (
            filtered
            + prototype[tap_index][None, None, :]
            * framed[:, first_input + tap_index : first_input + tap_index + count, :]
        )
    return filtered * antenna_flags.astype(jnp.float32)[:, None, None]


def transform_table():
    rows_int = jnp.arange(2 * CHANNEL_COUNT, dtype=jnp.int32)
    channel = rows_int // 2
    is_real = rows_int % 2 == 0
    sample = jnp.arange(NFFT, dtype=jnp.int32)
    phase = channel[:, None] * sample[None, :] % NFFT
    angle = 2 * jnp.pi * phase.astype(jnp.float32) / NFFT
    table = jnp.where(is_real[:, None], jnp.cos(angle), -jnp.sin(angle))
    return table / math.sqrt(NFFT)


def delay_table():
    chan_int = jnp.arange(CHANNEL_COUNT, dtype=jnp.int32)
    chan_float = chan_int.astype(jnp.float32)
    base = 2 * jnp.pi * chan_float / (CHANNEL_COUNT - 1)
    window = (
        0.35875
        - 0.48829 * jnp.cos(base)
        + 0.14128 * jnp.cos(2 * base)
        - 0.01168 * jnp.cos(3 * base)
    )
    phase = chan_int[:, None] * chan_int[None, :] % CHANNEL_COUNT
    angle = 2 * jnp.pi * phase.astype(jnp.float32) / CHANNEL_COUNT
    cosine = jnp.cos(angle) * window[None, :]
    sine = jnp.sin(angle) * window[None, :]
    upper = jnp.concatenate([cosine, sine], axis=1)
    lower = jnp.concatenate([-sine, cosine], axis=1)
    table = jnp.concatenate([upper, lower], axis=0) / jnp.sqrt(jnp.sum(window * window))
    return table.astype(jnp.bfloat16)


def plain_correlate(received):
    values = received[0]
    swapped = jnp.stack([values[:, 1], -values[:, 0]], axis=1)
    stacked = jnp.stack([values, swapped], axis=0)
    return jnp.einsum("qcrit,crjt->iqcj", stacked, values, preferred_element_type=jnp.float32)


def plain_device(voltages, antenna_flags, baseline_pairs):
    width = lax.axis_size("wide")
    local_inputs = voltages.shape[0]
    local_channels = CHANNEL_COUNT // width
    table = transform_table()
    scale = 1.0 / math.sqrt(2 * NT)
    correlation = jnp.zeros((INPUT_COUNT, 2, local_channels, INPUT_COUNT), jnp.float32)
    for batch_index in range(2):
        filtered = plain_filter_bank(voltages, antenna_flags, batch_index * NT, NT)
        raw = jnp.einsum(
            "kn,itn->kit",
            table,
            filtered,
            precision=lax.Precision.HIGHEST,
            preferred_element_type=jnp.float32,
        )
        correlation = correlation + plain_correlate(
            lax.all_to_all(
                raw.astype(jnp.bfloat16).reshape(width, local_channels, 2, local_inputs, NT),
                "wide",
                split_axis=0,
                concat_axis=3,
                tiled=True,
            )
        )
    baseline_count = baseline_pairs.shape[1]
    block_size = math.gcd(baseline_count, 1024)
    first_blocks = baseline_pairs[0].reshape(baseline_count // block_size, block_size)
    second_blocks = baseline_pairs[1].reshape(baseline_count // block_size, block_size)
    input_positions = jnp.arange(INPUT_COUNT, dtype=jnp.int32)

    def select_block(indices):
        first_block, second_block = indices
        rows_taken = jnp.take(correlation, first_block, axis=0)
        selector = (input_positions[None, :] == second_block[:, None]).astype(jnp.float32)
        return jnp.sum(rows_taken * selector[:, None, None, :], axis=3)

    selected = lax.map(select_block, (first_blocks, second_blocks))
    selected = selected.reshape(baseline_count, 2, local_channels)
    picked = (jnp.transpose(selected, (1, 2, 0)) * scale).astype(jnp.bfloat16)
    regrouped = lax.all_to_all(picked, "wide", split_axis=2, concat_axis=1, tiled=True)
    column_list = regrouped.reshape(2 * CHANNEL_COUNT, regrouped.shape[2])
    delays = jnp.dot(delay_table(), column_list, preferred_element_type=jnp.float32)
    return delays[:CHANNEL_COUNT] ** 2 + delays[CHANNEL_COUNT:] ** 2


def tiles(local_inputs, local_channels, count, width):
    fits = local_inputs % 16 == 0 and LANES % local_inputs == 0 and local_channels % 16 == 0
    return fits and count % BASE_TILE == 0 and (count // width) % LANES == 0


def per_device(voltages, antenna_flags, baseline_pairs):
    width = lax.axis_size("wide")
    local_inputs = voltages.shape[0]
    local_channels = CHANNEL_COUNT // width
    planes = 2 * local_channels
    count = baseline_pairs.shape[1]
    if not tiles(local_inputs, local_channels, count, width):
        return plain_device(voltages, antenna_flags, baseline_pairs)
    proto = jnp.asarray(prototype_np())
    even, odd = (jnp.asarray(transform_np(parity, width)) for parity in range(2))
    flags = antenna_flags.astype(jnp.float32)[:, None]
    inputs = lax.broadcasted_iota(jnp.int32, (INPUT_COUNT, count), 0)
    first = (inputs == baseline_pairs[0][None, :]).astype(jnp.bfloat16)
    second = (inputs == baseline_pairs[1][None, :]).astype(jnp.bfloat16)

    total = jnp.zeros((planes, count), jnp.float32)
    waiting = []
    start = 0
    for frames in CHUNKS:
        spectra = filter_bank(voltages, proto, flags, even, odd, start, frames, width)
        if len(waiting) > 1:
            total = correlate(waiting.pop(0), first, second, total)
            spectra, total = lax.optimization_barrier((spectra, total))
        received = lax.all_to_all(spectra, "wide", split_axis=0, concat_axis=0, tiled=True)
        waiting.append(received)
        start += frames
    for received in waiting:
        total = correlate(received, first, second, total)
    picked = (total * (1.0 / math.sqrt(FRAMES))).astype(jnp.bfloat16)
    picked = picked.reshape(planes, width, count // width).transpose(1, 0, 2)
    regrouped = lax.all_to_all(picked, "wide", split_axis=0, concat_axis=0, tiled=True)
    return delay_power(jnp.asarray(delay_np(width)), regrouped.reshape(2 * CHANNEL_COUNT, count // width))


def solution(mesh):
    placed = (P("wide", "groups"), P(("groups", "wide")), P())
    return jax.shard_map(
        per_device, mesh=mesh, in_specs=placed, out_specs=P("groups", "wide"), check_vma=False
    )
```

profile of v0, /device:TPU:0, one launch (start us, length us, event | category | flops | bytes accessed | tf_op | source)
XLA Modules:
  0.0 250.0 jit_solution(1627945638270976539)
XLA Ops:
  0.0 0.7 convert_bitcast_fusion
  0.7 0.1 copy.8.flag_ref
  0.7 0.0 copy-start
  0.8 3.4 %copy-done = bf16[32,132608]{1,0:T(8,128)(2,1)S(1)} copy-done((bf16[32,132608]{1,0:T(8,128)(2,1)S(1)}, bf16[32,132608]{1,0:T(8,128)(2,1)}, u32[]{:S(2)}) %copy-start) | copy-done | bytes 8486936
  4.2 0.0 copy-start.4
  4.2 1.0 copy-done.4
  5.2 0.0 copy-start.6
  5.2 1.0 copy-done.6
  6.2 0.0 copy-start.11
  6.2 0.7 copy-done.11
  6.8 9.1 %bank.4 = bf16[16,32,3072]{2,1,0:T(8,128)(2,1)} custom-call(bf16[32,132608]{1,0:T(8,128)(2,1)S(1)} %copy-done, bf16[32,132608]{1,0:T(8,128)(2,1)S(1)} %copy-done, bf16[32,132608]{1,0:T(8,128)(2,1)S(1)} %copy-done, bf16[32,132608]{1,0:T(8,128)(2,1)S(1)} %copy-done, f32[4,512]{1,0:T(4,128)S(1)} %copy-done.11, f32[32,1]{1,0:T(8,128)S(1)} %copy.8.flag_ref, ...), custom_call_target="tpu_custom_call" | custom-call | flops 2415919104 | bytes 6291456 | tf_op jit(solution)/shard_map/bank/pallas_call | solution.py:116
  16.0 0.0 copy-start.5
  16.0 0.0 copy-start.7
  16.0 0.0 copy-start.12
  16.0 7.6 %all-to-all-start = ((bf16[16,32,3072]{2,1,0:T(8,128)(2,1)}), bf16[16,32,3072]{2,1,0:T(8,128)(2,1)}, u32[]{:S(2)}, u32[]{:S(2)}) async-start(bf16[16,32,3072]{2,1,0:T(8,128)(2,1)} %bank.4), calls=%async_computation | async-start | bytes 6291456 | tf_op jit(solution)/shard_map/all_to_all | solution.py:343
  23.6 0.0 copy-done.5
  23.6 0.0 copy-done.7
  23.6 0.0 copy-done.12
  23.6 0.0 copy-start.1
  23.6 3.4 %copy-done.1 = bf16[32,132608]{1,0:T(8,128)(2,1)S(1)} copy-done((bf16[32,132608]{1,0:T(8,128)(2,1)S(1)}, bf16[32,132608]{1,0:T(8,128)(2,1)}, u32[]{:S(2)}) %copy-start.1) | copy-done | bytes 8486936
  27.0 11.3 %bank.5 = bf16[16,32,4096]{2,1,0:T(8,128)(2,1)S(1)} custom-call(bf16[32,132608]{1,0:T(8,128)(2,1)S(1)} %copy-done.1, bf16[32,132608]{1,0:T(8,128)(2,1)S(1)} %copy-done.1, bf16[32,132608]{1,0:T(8,128)(2,1)S(1)} %copy-done.1, bf16[32,132608]{1,0:T(8,128)(2,1)S(1)} %copy-done.1, f32[4,512]{1,0:T(4,128)S(1)} %copy-done.12, f32[32,1]{1,0:T(8,128)S(1)} %copy.8.flag_ref, ...), custom_call_target="tpu_custom_call" | custom-call | flops 3221225472 | bytes 8388608 | tf_op jit(solution)/shard_map/bank/pallas_call | solution.py:116
  38.4 0.0 copy-start.3
  38.4 2.0 copy-done.3
  40.4 42.5 %all-to-all-done.z_ref = bf16[16,32,3072]{2,1,0:T(8,128)(2,1)} async-done(((bf16[16,32,3072]{2,1,0:T(8,128)(2,1)}), bf16[16,32,3072]{2,1,0:T(8,128)(2,1)}, u32[]{:S(2)}, u32[]{:S(2)}) %all-to-all-start) | async-done | bytes 3145760 | tf_op jit(solution)/shard_map/all_to_all | solution.py:343
  82.9 15.5 %all-to-all-start.2 = ((bf16[16,32,4096]{2,1,0:T(8,128)(2,1)}), bf16[16,32,4096]{2,1,0:T(8,128)(2,1)}, u32[]{:S(2)}, u32[]{:S(2)}) async-start(bf16[16,32,4096]{2,1,0:T(8,128)(2,1)} %copy-done.3), calls=%async_computation.2 | async-start | bytes 8388608 | tf_op jit(solution)/shard_map/all_to_all | solution.py:343
  98.4 0.0 copy-start.2
  98.4 3.4 %copy-done.2 = bf16[32,132608]{1,0:T(8,128)(2,1)S(1)} copy-done((bf16[32,132608]{1,0:T(8,128)(2,1)S(1)}, bf16[32,132608]{1,0:T(8,128)(2,1)}, u32[]{:S(2)}) %copy-start.2) | copy-done | bytes 8486936
  101.8 0.0 copy-start.15
  101.8 3.5 %bank.3 = bf16[16,32,1024]{2,1,0:T(8,128)(2,1)} custom-call(bf16[32,132608]{1,0:T(8,128)(2,1)S(1)} %copy-done.2, bf16[32,132608]{1,0:T(8,128)(2,1)S(1)} %copy-done.2, bf16[32,132608]{1,0:T(8,128)(2,1)S(1)} %copy-done.2, bf16[32,132608]{1,0:T(8,128)(2,1)S(1)} %copy-done.2, f32[4,512]{1,0:T(4,128)S(1)} %copy-done.12, f32[32,1]{1,0:T(8,128)S(1)} %copy.8.flag_ref, ...), custom_call_target="tpu_custom_call" | custom-call | flops 805306368 | bytes 2097152 | tf_op jit(solution)/shard_map/bank/pallas_call | solution.py:116
  105.3 0.0 copy-done.15
  105.3 1.6 fusion
  106.9 21.2 %corr.3.past_ref = f32[32,2048]{1,0:T(8,128)S(1)} custom-call(bf16[16,32,3072]{2,1,0:T(8,128)(2,1)} %all-to-all-done.z_ref, bf16[512,2048]{1,0:T(8,128)(2,1)S(1)} %get-tuple-element.11.first_ref, bf16[512,2048]{1,0:T(8,128)(2,1)S(1)} %get-tuple-element.12.second_ref, f32[32,2048]{1,0:T(8,128)S(1)} %broadcast_in_dim.7.past_ref), custom_call_target="tpu_custom_call" | custom-call | flops 12884901888 | bytes 7340032 | tf_op jit(solution)/shard_map/corr/pallas_call | solution.py:175
  128.1 0.0 copy-start.8
  128.1 1.4 copy-done.8
  129.5 0.0 copy-start.13
  129.5 0.7 copy-done.13
  130.2 45.7 %all-to-all-done.2.z_ref = bf16[16,32,4096]{2,1,0:T(8,128)(2,1)} async-done(((bf16[16,32,4096]{2,1,0:T(8,128)(2,1)}), bf16[16,32,4096]{2,1,0:T(8,128)(2,1)}, u32[]{:S(2)}, u32[]{:S(2)}) %all-to-all-start.2) | async-done | bytes 4194336 | tf_op jit(solution)/shard_map/all_to_all | solution.py:343
  175.9 19.6 %all-to-all-start.1 = ((bf16[16,32,1024]{2,1,0:T(8,128)(2,1)}), bf16[16,32,1024]{2,1,0:T(8,128)(2,1)S(1)}, u32[]{:S(2)}, u32[]{:S(2)}) async-start(bf16[16,32,1024]{2,1,0:T(8,128)(2,1)} %bank.3), calls=%async_computation.1 | async-start | bytes 2097152 | tf_op jit(solution)/shard_map/all_to_all | solution.py:343
  195.6 0.0 copy-start.9
  195.6 1.6 copy-done.9
  197.1 0.0 copy-start.14
  197.1 0.9 copy-done.14
  198.1 27.8 %corr.4.past_ref = f32[32,2048]{1,0:T(8,128)S(1)} custom-call(bf16[16,32,4096]{2,1,0:T(8,128)(2,1)} %all-to-all-done.2.z_ref, bf16[512,2048]{1,0:T(8,128)(2,1)S(1)} %get-tuple-element.11.first_ref, bf16[512,2048]{1,0:T(8,128)(2,1)S(1)} %copy-done.9, f32[32,2048]{1,0:T(8,128)S(1)} %copy-done.14), custom_call_target="tpu_custom_call" | custom-call | flops 17179869184 | bytes 8388608 | tf_op jit(solution)/shard_map/corr/pallas_call | solution.py:175
  225.9 0.0 all-to-all-done.1.z_ref
  226.0 0.0 copy-start.10
  226.0 1.6 copy-done.10
  227.5 6.6 %corr.5 = f32[32,2048]{1,0:T(8,128)S(1)} custom-call(bf16[16,32,1024]{2,1,0:T(8,128)(2,1)S(1)} %all-to-all-done.1.z_ref, bf16[512,2048]{1,0:T(8,128)(2,1)S(1)} %get-tuple-element.11.first_ref, bf16[512,2048]{1,0:T(8,128)(2,1)S(1)} %copy-done.10, f32[32,2048]{1,0:T(8,128)S(1)} %corr.4.past_ref), custom_call_target="tpu_custom_call" | custom-call | flops 4294967296 | bytes 5242880 | tf_op jit(solution)/shard_map/corr/pallas_call | solution.py:175
  234.2 13.8 %all_to_all.20 = bf16[16,32,128]{2,1,0:T(8,128)(2,1)} all-to-all(bf16[16,32,128]{2,1,0:T(8,128)(2,1)S(1)} %bitcast_bitcast_fusion), channel_id=1, replica_groups=mesh['groups'=2,'wide'=16] {'wide'}, dimensions={0} | all-to-all | bytes 262144 | tf_op jit(solution)/shard_map/all_to_all | solution.py:350
  248.0 2.0 power.1
  (3 shorter events, 0.1 us)
Async XLA Ops:
  0.7 3.4 %copy-start = (bf16[32,132608]{1,0:T(8,128)(2,1)S(1)}, bf16[32,132608]{1,0:T(8,128)(2,1)}, u32[]{:S(2)}) copy-start(bf16[32,132608]{1,0:T(8,128)(2,1)} %h2_ref.5) | copy-start | bytes 25460740
  4.2 1.0 copy-start.4
  5.2 1.0 copy-start.6
  6.2 0.7 copy-start.11
  16.0 7.6 %copy-start.5 = (bf16[256,768]{1,0:T(8,128)(2,1)S(1)}, bf16[256,768]{1,0:T(8,128)(2,1)}, u32[]{:S(2)}) copy-start(bf16[256,768]{1,0:T(8,128)(2,1)} %constant.14.clone.odd_ref) | copy-start | bytes 1179652
  16.0 7.6 %copy-start.7 = (bf16[256,768]{1,0:T(8,128)(2,1)S(1)}, bf16[256,768]{1,0:T(8,128)(2,1)}, u32[]{:S(2)}) copy-start(bf16[256,768]{1,0:T(8,128)(2,1)} %constant.13.clone.even_ref) | copy-start | bytes 1179652
  16.0 7.6 %copy-start.12 = (f32[4,512]{1,0:T(4,128)S(1)}, f32[4,512]{1,0:T(4,128)}, u32[]{:S(2)}) copy-start(f32[4,512]{1,0:T(4,128)} %constant.12.clone.proto_ref) | copy-start | bytes 24580
  16.0 66.9 %all-to-all-start = ((bf16[16,32,3072]{2,1,0:T(8,128)(2,1)}), bf16[16,32,3072]{2,1,0:T(8,128)(2,1)}, u32[]{:S(2)}, u32[]{:S(2)}) async-start(bf16[16,32,3072]{2,1,0:T(8,128)(2,1)} %bank.4), calls=%async_computation | async-start | bytes 6291456 | tf_op jit(solution)/shard_map/all_to_all | solution.py:343
  23.6 3.4 %copy-start.1 = (bf16[32,132608]{1,0:T(8,128)(2,1)S(1)}, bf16[32,132608]{1,0:T(8,128)(2,1)}, u32[]{:S(2)}) copy-start(bf16[32,132608]{1,0:T(8,128)(2,1)} %h2_ref.5) | copy-start | bytes 25460740
  38.4 2.0 copy-start.3
  82.9 93.0 %all-to-all-start.2 = ((bf16[16,32,4096]{2,1,0:T(8,128)(2,1)}), bf16[16,32,4096]{2,1,0:T(8,128)(2,1)}, u32[]{:S(2)}, u32[]{:S(2)}) async-start(bf16[16,32,4096]{2,1,0:T(8,128)(2,1)} %copy-done.3), calls=%async_computation.2 | async-start | bytes 8388608 | tf_op jit(solution)/shard_map/all_to_all | solution.py:343
  98.4 3.4 %copy-start.2 = (bf16[32,132608]{1,0:T(8,128)(2,1)S(1)}, bf16[32,132608]{1,0:T(8,128)(2,1)}, u32[]{:S(2)}) copy-start(bf16[32,132608]{1,0:T(8,128)(2,1)} %h2_ref.5) | copy-start | bytes 25460740
  101.8 3.5 %copy-start.15 = (s32[2,2048]{1,0:T(2,128)S(1)}, s32[2,2048]{1,0:T(2,128)}, u32[]{:S(2)}) copy-start(s32[2,2048]{1,0:T(2,128)} %param.9) | copy-start | bytes 49156
  128.1 1.4 copy-start.8
  129.5 0.7 copy-start.13
  175.9 50.0 %all-to-all-start.1 = ((bf16[16,32,1024]{2,1,0:T(8,128)(2,1)}), bf16[16,32,1024]{2,1,0:T(8,128)(2,1)S(1)}, u32[]{:S(2)}, u32[]{:S(2)}) async-start(bf16[16,32,1024]{2,1,0:T(8,128)(2,1)} %bank.3), calls=%async_computation.1 | async-start | bytes 2097152 | tf_op jit(solution)/shard_map/all_to_all | solution.py:343
  195.6 1.6 copy-start.9
  197.1 0.9 copy-start.14
  226.0 1.6 copy-start.10
where the time goes:
time: 251 us; the launch traced here: 250 us
  waiting for transfers between devices  88.2 us (35%)
  Pallas kernels  81.7 us (33%)
  starting transfers between devices  42.7 us (17%)
  local copies, waits for them, and re-layouts  21.2 us (8%)
  blocking collectives  13.8 us (5%)
    all_to_all x3, waiting for transfers between devices, per_device(): lax.all_to_all(spectra, 'wide', split_axis=0, concat_axis=0, tiled=True)  88.2 us
    pallas_call x3, Pallas kernels, correlate(): pl.pallas_call(corr_kernel, grid=(lanes // step_lanes,), in_specs=[pl.Blo...  55.7 us
    all_to_all x3, starting transfers between devices, per_device(): lax.all_to_all(spectra, 'wide', split_axis=0, concat_axis=0, tiled=True)  42.7 us
    pallas_call x3, Pallas kernels, filter_bank(): pl.pallas_call(bank_kernel, grid=(count // BANK_STEP,), in_specs=[main, *...  24 us
    unnamed x32, local copies, waits for them, and re-layouts  21.1 us
    all_to_all x1, blocking collectives, per_device(): lax.all_to_all(picked, 'wide', split_axis=0, concat_axis=0, tiled=True)  13.8 us
  transfers between devices with their start and end apart: 3, of which 2 were waited for; matrix products, arithmetic and copies ran while one was open for 1% of the time, Pallas kernels for 26%

commit v1 on v0

--- a/solution.py
+++ b/solution.py
@@ -16,9 +16,11 @@
 HALF = NFFT // 2
 FRAMES = 2 * NT
 
-CHUNKS = (96, 128, 32)
+CHUNKS = (32, 128, 72, 24)
 BANK_STEP = 8
 CORR_STEP = 32
+GRANT = 58 * 2**20
+CORR_GRANT = 32 * 2**20
 LANES = 128
 BASE_TILE = 256
 
@@ -70,8 +72,11 @@
             return x_ref[at : at + rows, t * NFFT + column : t * NFFT + column + LANES].astype(jnp.float32)
         return halo[t - BANK_STEP][at : at + rows, column : column + LANES].astype(jnp.float32)
 
+    here = lax.broadcasted_iota(jnp.int32, (rows, inputs), 0)
+    there = lax.broadcasted_iota(jnp.int32, (rows, inputs), 1)
     for at in range(0, inputs, rows):
-        flag = flag_ref[at : at + rows, :]
+        flag = jnp.where(here + at == there, flag_ref[...].astype(jnp.float32), 0.0)
+        flag = jnp.sum(flag, axis=1, keepdims=True)
         for column in range(0, HALF, LANES):
             parts = []
             for side in (column, column + HALF):
@@ -120,7 +125,7 @@
         out_specs=pl.BlockSpec((width, 2 * local, step_lanes), lambda j: (0, 0, j)),
         out_shape=jax.ShapeDtypeStruct((width, 2 * local, count * inputs), jnp.bfloat16),
         scratch_shapes=[pltpu.VMEM((step_lanes, 3 * HALF), jnp.bfloat16)] * 2,
-        compiler_params=pltpu.CompilerParams(vmem_limit_bytes=32 * 2**20),
+        compiler_params=pltpu.CompilerParams(vmem_limit_bytes=GRANT),
         cost_estimate=pl.CostEstimate(
             flops=2 * 3 * count * inputs * NFFT * HALF, bytes_accessed=4 * count * inputs * NFFT, transcendentals=0
         ),
@@ -128,7 +133,7 @@
     )(voltages, voltages, voltages, voltages, proto, flags, even, odd)
 
 
-def corr_kernel(z_ref, first_ref, second_ref, past_ref, out_ref, rows_ref):
+def corr_kernel(z_ref, pairs_ref, past_ref, out_ref, rows_ref, first_ref, second_ref):
     sources, planes, lanes = z_ref.shape
     inputs = INPUT_COUNT // sources
     group = LANES // inputs
@@ -140,6 +145,16 @@
     @pl.when(step == 0)
     def _():
         out_ref[...] = past_ref[...]
+        index = lax.broadcasted_iota(jnp.int32, (INPUT_COUNT, BASE_TILE), 0)
+
+        def select(k, carry):
+            at = pl.ds(pl.multiple_of(k * BASE_TILE, BASE_TILE), BASE_TILE)
+            for row, ref in enumerate((first_ref, second_ref)):
+                hit = index == pairs_ref[row : row + 1, at]
+                ref[:, at] = jnp.where(hit, 1.0, 0.0).astype(jnp.bfloat16)
+            return carry
+
+        lax.fori_loop(0, pairs_ref.shape[1] // BASE_TILE, select, 0)
 
     for block in range(lanes // LANES):
         for lead in range(0, sources, group):
@@ -166,32 +181,36 @@
     lax.fori_loop(0, first_ref.shape[1] // BASE_TILE, tile, 0)
 
 
-def correlate(received, first, second, past):
+def correlate(received, pairs, past):
     sources, planes, lanes = received.shape
     inputs = INPUT_COUNT // sources
-    step_lanes = CORR_STEP * inputs
-    count = first.shape[1]
+    frames = lanes // inputs
+    per_step = max(f for f in range(BANK_STEP, CORR_STEP + 1, BANK_STEP) if frames % f == 0)
+    count = pairs.shape[1]
     whole = lambda a: pl.BlockSpec(a.shape, lambda j: (0, 0))
     return pl.pallas_call(
         corr_kernel,
-        grid=(lanes // step_lanes,),
+        grid=(frames // per_step,),
         in_specs=[
-            pl.BlockSpec((sources, planes, step_lanes), lambda j: (0, 0, j)),
-            whole(first),
-            whole(second),
+            pl.BlockSpec((sources, planes, per_step * inputs), lambda j: (0, 0, j)),
+            whole(pairs),
             whole(past),
         ],
         out_specs=pl.BlockSpec((planes, count), lambda j: (0, 0)),
         out_shape=jax.ShapeDtypeStruct((planes, count), jnp.float32),
-        scratch_shapes=[pltpu.VMEM((CORR_STEP * planes, INPUT_COUNT), jnp.bfloat16)],
-        compiler_params=pltpu.CompilerParams(vmem_limit_bytes=48 * 2**20),
+        scratch_shapes=[
+            pltpu.VMEM((per_step * planes, INPUT_COUNT), jnp.bfloat16),
+            pltpu.VMEM((INPUT_COUNT, count), jnp.bfloat16),
+            pltpu.VMEM((INPUT_COUNT, count), jnp.bfloat16),
+        ],
+        compiler_params=pltpu.CompilerParams(vmem_limit_bytes=CORR_GRANT),
         cost_estimate=pl.CostEstimate(
-            flops=4 * (lanes // inputs) * planes * INPUT_COUNT * count,
-            bytes_accessed=2 * sources * planes * lanes + 4 * INPUT_COUNT * count,
+            flops=4 * frames * planes * INPUT_COUNT * count,
+            bytes_accessed=2 * sources * planes * lanes,
             transcendentals=0,
         ),
         name="corr",
-    )(received, first, second, past)
+    )(received, pairs, past)
 
 
 def power_kernel(table_ref, values_ref, out_ref):
@@ -327,10 +346,7 @@
         return plain_device(voltages, antenna_flags, baseline_pairs)
     proto = jnp.asarray(prototype_np())
     even, odd = (jnp.asarray(transform_np(parity, width)) for parity in range(2))
-    flags = antenna_flags.astype(jnp.float32)[:, None]
-    inputs = lax.broadcasted_iota(jnp.int32, (INPUT_COUNT, count), 0)
-    first = (inputs == baseline_pairs[0][None, :]).astype(jnp.bfloat16)
-    second = (inputs == baseline_pairs[1][None, :]).astype(jnp.bfloat16)
+    flags = antenna_flags[None, :]
 
     total = jnp.zeros((planes, count), jnp.float32)
     waiting = []
@@ -338,13 +354,13 @@
     for frames in CHUNKS:
         spectra = filter_bank(voltages, proto, flags, even, odd, start, frames, width)
         if len(waiting) > 1:
-            total = correlate(waiting.pop(0), first, second, total)
+            total = correlate(waiting.pop(0), baseline_pairs, total)
             spectra, total = lax.optimization_barrier((spectra, total))
         received = lax.all_to_all(spectra, "wide", split_axis=0, concat_axis=0, tiled=True)
         waiting.append(received)
         start += frames
     for received in waiting:
-        total = correlate(received, first, second, total)
+        total = correlate(received, baseline_pairs, total)
     picked = (total * (1.0 / math.sqrt(FRAMES))).astype(jnp.bfloat16)
     picked = picked.reshape(planes, width, count // width).transpose(1, 0, 2)
     regrouped = lax.all_to_all(picked, "wide", split_axis=0, concat_axis=0, tiled=True)

time: 251 us -> 238 us (0.948)
  local copies, waits for them, and re-layouts: 21.2 us -> 1.66 us
  Pallas kernels: 81.7 us -> 95.4 us
  waiting for transfers between devices: 88.2 us -> 80.7 us
  starting transfers between devices: 42.7 us -> 46.2 us
    unnamed x32 -> x6, local copies, waits for them, and re-layouts: 21.1 us -> 1.65 us
    pallas_call x3 -> x4, Pallas kernels: 24 us -> 34.1 us  [filter_bank(): pl.pallas_call(bank_kernel, grid=(count // BANK_STEP,), in_specs=[main, *...]
    all_to_all x3 -> x4, waiting for transfers between devices: 88.2 us -> 80.7 us  [per_device(): lax.all_to_all(spectra, 'wide', split_axis=0, concat_axis=0, tiled=True)]
    pallas_call x3 -> x4, Pallas kernels: 55.7 us -> 59.3 us  [correlate(): pl.pallas_call(corr_kernel, grid=(frames // per_step,), in_specs=[pl.Bloc...]
    all_to_all x3 -> x4, starting transfers between devices: 42.7 us -> 46.2 us  [per_device(): lax.all_to_all(spectra, 'wide', split_axis=0, concat_axis=0, tiled=True)]
  transfers between devices with their start and end apart: 3 -> 4, of which waited for: 2 -> 4; matrix products, arithmetic and copies ran while one was open for 1% -> 0% of each run, Pallas kernels for 26% -> 35%
where the time goes in v1:
time: 238 us; the launch traced here: 237 us
  Pallas kernels  95.4 us (40%)
  waiting for transfers between devices  80.7 us (34%)
  starting transfers between devices  46.2 us (19%)
  blocking collectives  13.2 us (6%)
    all_to_all x4, waiting for transfers between devices, per_device(): lax.all_to_all(spectra, 'wide', split_axis=0, concat_axis=0, tiled=True)  80.7 us
    pallas_call x4, Pallas kernels, correlate(): pl.pallas_call(corr_kernel, grid=(frames // per_step,), in_specs=[pl.Bloc...  59.3 us
    all_to_all x4, starting transfers between devices, per_device(): lax.all_to_all(spectra, 'wide', split_axis=0, concat_axis=0, tiled=True)  46.2 us
    pallas_call x4, Pallas kernels, filter_bank(): pl.pallas_call(bank_kernel, grid=(count // BANK_STEP,), in_specs=[main, *...  34.1 us
    all_to_all x1, blocking collectives, per_device(): lax.all_to_all(picked, 'wide', split_axis=0, concat_axis=0, tiled=True)  13.2 us
  transfers between devices with their start and end apart: 4, of which 4 were waited for; matrix products, arithmetic and copies ran while one was open for 0% of the time, Pallas kernels for 35%

profile of v1, /device:TPU:0, one launch (start us, length us, event | category | flops | bytes accessed | tf_op | source)
XLA Modules:
  0.0 237.3 jit_solution(16098112694720229955)
XLA Ops:
  0.0 5.0 %bank.7 = bf16[16,32,1024]{2,1,0:T(8,128)(2,1)} custom-call(bf16[32,132608]{1,0:T(8,128)(2,1)} %h2_ref.7, bf16[32,132608]{1,0:T(8,128)(2,1)} %h2_ref.7, bf16[32,132608]{1,0:T(8,128)(2,1)} %h2_ref.7, bf16[32,132608]{1,0:T(8,128)(2,1)} %h2_ref.7, f32[4,512]{1,0:T(4,128)} %constant.12.clone.proto_ref, s32[1,32]{1,0:T(1,128)} %bitcast.10, ...), custom_call_target="tpu_custom_call" | custom-call | flops 805306368 | bytes 2097152 | tf_op jit(solution)/shard_map/bank/pallas_call | solution.py:121
  5.0 7.5 %all-to-all-start.1 = ((bf16[16,32,1024]{2,1,0:T(8,128)(2,1)}), bf16[16,32,1024]{2,1,0:T(8,128)(2,1)S(1)}, u32[]{:S(2)}, u32[]{:S(2)}) async-start(bf16[16,32,1024]{2,1,0:T(8,128)(2,1)} %bank.7), calls=%async_computation.1 | async-start | bytes 2097152 | tf_op jit(solution)/shard_map/all_to_all | solution.py:359
  12.5 15.3 %bank.5 = bf16[16,32,4096]{2,1,0:T(8,128)(2,1)} custom-call(bf16[32,132608]{1,0:T(8,128)(2,1)} %h2_ref.7, bf16[32,132608]{1,0:T(8,128)(2,1)} %h2_ref.7, bf16[32,132608]{1,0:T(8,128)(2,1)} %h2_ref.7, bf16[32,132608]{1,0:T(8,128)(2,1)} %h2_ref.7, f32[4,512]{1,0:T(4,128)} %constant.12.clone.proto_ref, s32[1,32]{1,0:T(1,128)} %bitcast.11, ...), custom_call_target="tpu_custom_call" | custom-call | flops 3221225472 | bytes 8388608 | tf_op jit(solution)/shard_map/bank/pallas_call | solution.py:121
  27.8 7.6 %all-to-all-done.1.z_ref = bf16[16,32,1024]{2,1,0:T(8,128)(2,1)S(1)} async-done(((bf16[16,32,1024]{2,1,0:T(8,128)(2,1)}), bf16[16,32,1024]{2,1,0:T(8,128)(2,1)S(1)}, u32[]{:S(2)}, u32[]{:S(2)}) %all-to-all-start.1) | async-done | bytes 1048608 | tf_op jit(solution)/shard_map/all_to_all | solution.py:359
  35.4 6.8 %all-to-all-start = ((bf16[16,32,4096]{2,1,0:T(8,128)(2,1)}), bf16[16,32,4096]{2,1,0:T(8,128)(2,1)}, u32[]{:S(2)}, u32[]{:S(2)}) async-start(bf16[16,32,4096]{2,1,0:T(8,128)(2,1)} %bank.5), calls=%async_computation | async-start | bytes 8388608 | tf_op jit(solution)/shard_map/all_to_all | solution.py:359
  42.2 0.0 copy-start
  42.2 9.5 %bank.6 = bf16[16,32,2304]{2,1,0:T(8,128)(2,1)} custom-call(bf16[32,132608]{1,0:T(8,128)(2,1)} %h2_ref.7, bf16[32,132608]{1,0:T(8,128)(2,1)} %h2_ref.7, bf16[32,132608]{1,0:T(8,128)(2,1)} %h2_ref.7, bf16[32,132608]{1,0:T(8,128)(2,1)} %h2_ref.7, f32[4,512]{1,0:T(4,128)} %constant.12.clone.proto_ref, s32[1,32]{1,0:T(1,128)} %bitcast.12, ...), custom_call_target="tpu_custom_call" | custom-call | flops 1811939328 | bytes 4718592 | tf_op jit(solution)/shard_map/bank/pallas_call | solution.py:121
  51.7 0.0 copy-done
  51.7 7.4 %corr.4.past_ref = f32[32,2048]{1,0:T(8,128)S(1)} custom-call(bf16[16,32,1024]{2,1,0:T(8,128)(2,1)S(1)} %all-to-all-done.1.z_ref, s32[2,2048]{1,0:T(2,128)S(1)} %copy-done, f32[32,2048]{1,0:T(8,128)S(1)} %broadcast_in_dim.7.past_ref), custom_call_target="tpu_custom_call" | custom-call | flops 4294967296 | bytes 1048576 | tf_op jit(solution)/shard_map/corr/pallas_call | solution.py:191
  59.2 60.6 %all-to-all-done.z_ref = bf16[16,32,4096]{2,1,0:T(8,128)(2,1)} async-done(((bf16[16,32,4096]{2,1,0:T(8,128)(2,1)}), bf16[16,32,4096]{2,1,0:T(8,128)(2,1)}, u32[]{:S(2)}, u32[]{:S(2)}) %all-to-all-start) | async-done | bytes 4194336 | tf_op jit(solution)/shard_map/all_to_all | solution.py:359
  119.8 19.6 %all-to-all-start.3 = ((bf16[16,32,2304]{2,1,0:T(8,128)(2,1)}), bf16[16,32,2304]{2,1,0:T(8,128)(2,1)S(1)}, u32[]{:S(2)}, u32[]{:S(2)}) async-start(bf16[16,32,2304]{2,1,0:T(8,128)(2,1)} %bank.6), calls=%async_computation.3 | async-start | bytes 4718592 | tf_op jit(solution)/shard_map/all_to_all | solution.py:359
  139.4 4.4 %bank.4 = bf16[16,32,768]{2,1,0:T(8,128)(2,1)} custom-call(bf16[32,132608]{1,0:T(8,128)(2,1)} %h2_ref.7, bf16[32,132608]{1,0:T(8,128)(2,1)} %h2_ref.7, bf16[32,132608]{1,0:T(8,128)(2,1)} %h2_ref.7, bf16[32,132608]{1,0:T(8,128)(2,1)} %h2_ref.7, f32[4,512]{1,0:T(4,128)} %constant.12.clone.proto_ref, s32[1,32]{1,0:T(1,128)} %bitcast.13, ...), custom_call_target="tpu_custom_call" | custom-call | flops 603979776 | bytes 1572864 | tf_op jit(solution)/shard_map/bank/pallas_call | solution.py:121
  143.8 28.6 %corr.5.past_ref = f32[32,2048]{1,0:T(8,128)S(1)} custom-call(bf16[16,32,4096]{2,1,0:T(8,128)(2,1)} %all-to-all-done.z_ref, s32[2,2048]{1,0:T(2,128)S(1)} %copy-done, f32[32,2048]{1,0:T(8,128)S(1)} %corr.4.past_ref), custom_call_target="tpu_custom_call" | custom-call | flops 17179869184 | bytes 4194304 | tf_op jit(solution)/shard_map/corr/pallas_call | solution.py:191
  172.4 0.0 copy-start.1
  172.4 0.7 copy-done.1
  173.1 11.8 %all-to-all-done.3.z_ref = bf16[16,32,2304]{2,1,0:T(8,128)(2,1)S(1)} async-done(((bf16[16,32,2304]{2,1,0:T(8,128)(2,1)}), bf16[16,32,2304]{2,1,0:T(8,128)(2,1)S(1)}, u32[]{:S(2)}, u32[]{:S(2)}) %all-to-all-start.3) | async-done | bytes 2359328 | tf_op jit(solution)/shard_map/all_to_all | solution.py:359
  185.0 12.3 %all-to-all-start.2 = ((bf16[16,32,768]{2,1,0:T(8,128)(2,1)}), bf16[16,32,768]{2,1,0:T(8,128)(2,1)S(1)}, u32[]{:S(2)}, u32[]{:S(2)}) async-start(bf16[16,32,768]{2,1,0:T(8,128)(2,1)} %bank.4), calls=%async_computation.2 | async-start | bytes 1572864 | tf_op jit(solution)/shard_map/all_to_all | solution.py:359
  197.2 0.0 copy-start.2
  197.3 0.9 copy-done.2
  198.2 17.1 %corr.6.past_ref = f32[32,2048]{1,0:T(8,128)S(1)} custom-call(bf16[16,32,2304]{2,1,0:T(8,128)(2,1)S(1)} %all-to-all-done.3.z_ref, s32[2,2048]{1,0:T(2,128)S(1)} %copy-done, f32[32,2048]{1,0:T(8,128)S(1)} %copy-done.2), custom_call_target="tpu_custom_call" | custom-call | flops 9663676416 | bytes 2359296 | tf_op jit(solution)/shard_map/corr/pallas_call | solution.py:191
  215.3 0.7 all-to-all-done.2.z_ref
  215.9 6.1 %corr.7 = f32[32,2048]{1,0:T(8,128)S(1)} custom-call(bf16[16,32,768]{2,1,0:T(8,128)(2,1)S(1)} %all-to-all-done.2.z_ref, s32[2,2048]{1,0:T(2,128)S(1)} %copy-done, f32[32,2048]{1,0:T(8,128)S(1)} %corr.6.past_ref), custom_call_target="tpu_custom_call" | custom-call | flops 3221225472 | bytes 786432 | tf_op jit(solution)/shard_map/corr/pallas_call | solution.py:191
  222.1 13.2 %all_to_all.25 = bf16[16,32,128]{2,1,0:T(8,128)(2,1)} all-to-all(bf16[16,32,128]{2,1,0:T(8,128)(2,1)S(1)} %bitcast_bitcast_fusion), channel_id=1, replica_groups=mesh['groups'=2,'wide'=16] {'wide'}, dimensions={0} | all-to-all | bytes 262144 | tf_op jit(solution)/shard_map/all_to_all | solution.py:366
  235.3 2.0 power.1
  (2 shorter events, 0.0 us)
Async XLA Ops:
  5.0 30.4 %all-to-all-start.1 = ((bf16[16,32,1024]{2,1,0:T(8,128)(2,1)}), bf16[16,32,1024]{2,1,0:T(8,128)(2,1)S(1)}, u32[]{:S(2)}, u32[]{:S(2)}) async-start(bf16[16,32,1024]{2,1,0:T(8,128)(2,1)} %bank.7), calls=%async_computation.1 | async-start | bytes 2097152 | tf_op jit(solution)/shard_map/all_to_all | solution.py:359
  35.4 84.4 %all-to-all-start = ((bf16[16,32,4096]{2,1,0:T(8,128)(2,1)}), bf16[16,32,4096]{2,1,0:T(8,128)(2,1)}, u32[]{:S(2)}, u32[]{:S(2)}) async-start(bf16[16,32,4096]{2,1,0:T(8,128)(2,1)} %bank.5), calls=%async_computation | async-start | bytes 8388608 | tf_op jit(solution)/shard_map/all_to_all | solution.py:359
  42.2 9.5 %copy-start = (s32[2,2048]{1,0:T(2,128)S(1)}, s32[2,2048]{1,0:T(2,128)}, u32[]{:S(2)}) copy-start(s32[2,2048]{1,0:T(2,128)} %pairs_ref.7) | copy-start | bytes 49156
  119.8 65.2 %all-to-all-start.3 = ((bf16[16,32,2304]{2,1,0:T(8,128)(2,1)}), bf16[16,32,2304]{2,1,0:T(8,128)(2,1)S(1)}, u32[]{:S(2)}, u32[]{:S(2)}) async-start(bf16[16,32,2304]{2,1,0:T(8,128)(2,1)} %bank.6), calls=%async_computation.3 | async-start | bytes 4718592 | tf_op jit(solution)/shard_map/all_to_all | solution.py:359
  172.4 0.7 copy-start.1
  185.0 31.0 %all-to-all-start.2 = ((bf16[16,32,768]{2,1,0:T(8,128)(2,1)}), bf16[16,32,768]{2,1,0:T(8,128)(2,1)S(1)}, u32[]{:S(2)}, u32[]{:S(2)}) async-start(bf16[16,32,768]{2,1,0:T(8,128)(2,1)} %bank.4), calls=%async_computation.2 | async-start | bytes 1572864 | tf_op jit(solution)/shard_map/all_to_all | solution.py:359
  197.2 1.0 copy-start.2

commit v2 on v1

--- a/solution.py
+++ b/solution.py
@@ -16,13 +16,15 @@
 HALF = NFFT // 2
 FRAMES = 2 * NT
 
-CHUNKS = (32, 128, 72, 24)
+CHUNKS = (32, 144, 56, 24)
 BANK_STEP = 8
 CORR_STEP = 32
-GRANT = 58 * 2**20
-CORR_GRANT = 32 * 2**20
+BANK_GRANT = 58 * 2**20
+CORR_GRANT = 28 * 2**20
+POWER_GRANT = 8 * 2**20
 LANES = 128
 BASE_TILE = 256
+UNROLL = 2
 
 
 def prototype_np():
@@ -125,7 +127,7 @@
         out_specs=pl.BlockSpec((width, 2 * local, step_lanes), lambda j: (0, 0, j)),
         out_shape=jax.ShapeDtypeStruct((width, 2 * local, count * inputs), jnp.bfloat16),
         scratch_shapes=[pltpu.VMEM((step_lanes, 3 * HALF), jnp.bfloat16)] * 2,
-        compiler_params=pltpu.CompilerParams(vmem_limit_bytes=GRANT),
+        compiler_params=pltpu.CompilerParams(vmem_limit_bytes=BANK_GRANT),
         cost_estimate=pl.CostEstimate(
             flops=2 * 3 * count * inputs * NFFT * HALF, bytes_accessed=4 * count * inputs * NFFT, transcendentals=0
         ),
@@ -133,7 +135,7 @@
     )(voltages, voltages, voltages, voltages, proto, flags, even, odd)
 
 
-def corr_kernel(z_ref, pairs_ref, past_ref, out_ref, rows_ref, first_ref, second_ref):
+def corr_kernel(z_ref, pairs_ref, past_ref, out_ref, rows_ref):
     sources, planes, lanes = z_ref.shape
     inputs = INPUT_COUNT // sources
     group = LANES // inputs
@@ -145,16 +147,6 @@
     @pl.when(step == 0)
     def _():
         out_ref[...] = past_ref[...]
-        index = lax.broadcasted_iota(jnp.int32, (INPUT_COUNT, BASE_TILE), 0)
-
-        def select(k, carry):
-            at = pl.ds(pl.multiple_of(k * BASE_TILE, BASE_TILE), BASE_TILE)
-            for row, ref in enumerate((first_ref, second_ref)):
-                hit = index == pairs_ref[row : row + 1, at]
-                ref[:, at] = jnp.where(hit, 1.0, 0.0).astype(jnp.bfloat16)
-            return carry
-
-        lax.fori_loop(0, pairs_ref.shape[1] // BASE_TILE, select, 0)
 
     for block in range(lanes // LANES):
         for lead in range(0, sources, group):
@@ -164,10 +156,18 @@
                 at = (block * group + t) * planes
                 rows_ref[at : at + planes, lead * inputs : lead * inputs + LANES] = joined
 
+    index = lax.broadcasted_iota(jnp.int32, (INPUT_COUNT, BASE_TILE), 0)
+
     def tile(k, carry):
         at = pl.ds(pl.multiple_of(k * BASE_TILE, BASE_TILE), BASE_TILE)
-        first = jnp.dot(rows_ref[...], first_ref[:, at], preferred_element_type=jnp.float32)
-        second = jnp.dot(rows_ref[...], second_ref[:, at], preferred_element_type=jnp.float32)
+        first, second = (
+            jnp.dot(
+                rows_ref[...],
+                jnp.where(index == pairs_ref[row : row + 1, at], 1.0, 0.0).astype(jnp.bfloat16),
+                preferred_element_type=jnp.float32,
+            )
+            for row in range(2)
+        )
         first = first.reshape(frames, 2, 2, eighth, BASE_TILE)
         second = second.reshape(frames, 2, 2, eighth, BASE_TILE)
         real = jnp.sum(first[:, :, 0] * second[:, :, 0] + first[:, :, 1] * second[:, :, 1], axis=0)
@@ -178,14 +178,14 @@
             out_ref[base + eighth : base + half, at] += imag[parity]
         return carry
 
-    lax.fori_loop(0, first_ref.shape[1] // BASE_TILE, tile, 0)
+    lax.fori_loop(0, pairs_ref.shape[1] // BASE_TILE, tile, 0, unroll=UNROLL)
 
 
 def correlate(received, pairs, past):
     sources, planes, lanes = received.shape
     inputs = INPUT_COUNT // sources
     frames = lanes // inputs
-    per_step = max(f for f in range(BANK_STEP, CORR_STEP + 1, BANK_STEP) if frames % f == 0)
+    per_step = max(f for f in range(4, CORR_STEP + 1, 4) if frames % f == 0)
     count = pairs.shape[1]
     whole = lambda a: pl.BlockSpec(a.shape, lambda j: (0, 0))
     return pl.pallas_call(
@@ -196,13 +196,9 @@
             whole(pairs),
             whole(past),
         ],
-        out_specs=pl.BlockSpec((planes, count), lambda j: (0, 0)),
-        out_shape=jax.ShapeDtypeStruct((planes, count), jnp.float32),
-        scratch_shapes=[
-            pltpu.VMEM((per_step * planes, INPUT_COUNT), jnp.bfloat16),
-            pltpu.VMEM((INPUT_COUNT, count), jnp.bfloat16),
-            pltpu.VMEM((INPUT_COUNT, count), jnp.bfloat16),
-        ],
+        out_specs=whole(past),
+        out_shape=jax.ShapeDtypeStruct(past.shape, jnp.float32),
+        scratch_shapes=[pltpu.VMEM((per_step * planes, INPUT_COUNT), jnp.bfloat16)],
         compiler_params=pltpu.CompilerParams(vmem_limit_bytes=CORR_GRANT),
         cost_estimate=pl.CostEstimate(
             flops=4 * frames * planes * INPUT_COUNT * count,
@@ -222,6 +218,7 @@
     return pl.pallas_call(
         power_kernel,
         out_shape=jax.ShapeDtypeStruct((CHANNEL_COUNT, values.shape[1]), jnp.float32),
+        compiler_params=pltpu.CompilerParams(vmem_limit_bytes=POWER_GRANT),
         name="power",
     )(table, values)
 
@@ -347,7 +344,6 @@
     proto = jnp.asarray(prototype_np())
     even, odd = (jnp.asarray(transform_np(parity, width)) for parity in range(2))
     flags = antenna_flags[None, :]
-
     total = jnp.zeros((planes, count), jnp.float32)
     waiting = []
     start = 0
@@ -356,8 +352,7 @@
         if len(waiting) > 1:
             total = correlate(waiting.pop(0), baseline_pairs, total)
             spectra, total = lax.optimization_barrier((spectra, total))
-        received = lax.all_to_all(spectra, "wide", split_axis=0, concat_axis=0, tiled=True)
-        waiting.append(received)
+        waiting.append(lax.all_to_all(spectra, "wide", split_axis=0, concat_axis=0, tiled=True))
         start += frames
     for received in waiting:
         total = correlate(received, baseline_pairs, total)

time: 238 us -> 236 us (level)
  Pallas kernels: 95.4 us -> 85.8 us
  waiting for transfers between devices: 80.7 us -> 89.4 us
    all_to_all x4, waiting for transfers between devices: 80.7 us -> 89.4 us  [per_device(): lax.all_to_all(spectra, 'wide', split_axis=0, concat_axis=0, tiled=True)]
    pallas_call x4, Pallas kernels: 59.3 us -> 50.7 us  [correlate(): pl.pallas_call(corr_kernel, grid=(frames // per_step,), in_specs=[pl.Bloc...]
  transfers between devices with their start and end apart: 4 -> 4, of which waited for: 4 -> 4; matrix products, arithmetic and copies ran while one was open for 0% -> 0% of each run, Pallas kernels for 35% -> 32%
where the time goes in v2:
time: 236 us; the launch traced here: 235 us
  waiting for transfers between devices  89.4 us (38%)
  Pallas kernels  85.8 us (36%)
  starting transfers between devices  46.2 us (20%)
  blocking collectives  13.1 us (6%)
    all_to_all x4, waiting for transfers between devices, per_device(): lax.all_to_all(spectra, 'wide', split_axis=0, concat_axis=0, tiled=True)  89.4 us
    pallas_call x4, Pallas kernels, correlate(): pl.pallas_call(corr_kernel, grid=(frames // per_step,), in_specs=[pl.Bloc...  50.7 us
    all_to_all x4, starting transfers between devices, per_device(): lax.all_to_all(spectra, 'wide', split_axis=0, concat_axis=0, tiled=True)  46.2 us
    pallas_call x4, Pallas kernels, filter_bank(): pl.pallas_call(bank_kernel, grid=(count // BANK_STEP,), in_specs=[main, *...  34.2 us
    all_to_all x1, blocking collectives, per_device(): lax.all_to_all(picked, 'wide', split_axis=0, concat_axis=0, tiled=True)  13.1 us
  transfers between devices with their start and end apart: 4, of which 4 were waited for; matrix products, arithmetic and copies ran while one was open for 0% of the time, Pallas kernels for 32%

profile of v2, /device:TPU:0, one launch (start us, length us, event | category | flops | bytes accessed | tf_op | source)
XLA Modules:
  0.0 234.7 jit_solution(18054791242243904781)
XLA Ops:
  0.0 5.0 %bank.7 = bf16[16,32,1024]{2,1,0:T(8,128)(2,1)} custom-call(bf16[32,132608]{1,0:T(8,128)(2,1)} %h2_ref.7, bf16[32,132608]{1,0:T(8,128)(2,1)} %h2_ref.7, bf16[32,132608]{1,0:T(8,128)(2,1)} %h2_ref.7, bf16[32,132608]{1,0:T(8,128)(2,1)} %h2_ref.7, f32[4,512]{1,0:T(4,128)} %constant.12.clone.proto_ref, s32[1,32]{1,0:T(1,128)} %bitcast.10, ...), custom_call_target="tpu_custom_call" | custom-call | flops 805306368 | bytes 2097152 | tf_op jit(solution)/shard_map/bank/pallas_call | solution.py:123
  5.0 7.5 %all-to-all-start.1 = ((bf16[16,32,1024]{2,1,0:T(8,128)(2,1)}), bf16[16,32,1024]{2,1,0:T(8,128)(2,1)S(1)}, u32[]{:S(2)}, u32[]{:S(2)}) async-start(bf16[16,32,1024]{2,1,0:T(8,128)(2,1)} %bank.7), calls=%async_computation.1 | async-start | bytes 2097152 | tf_op jit(solution)/shard_map/all_to_all | solution.py:355
  12.5 17.0 %bank.5 = bf16[16,32,4608]{2,1,0:T(8,128)(2,1)} custom-call(bf16[32,132608]{1,0:T(8,128)(2,1)} %h2_ref.7, bf16[32,132608]{1,0:T(8,128)(2,1)} %h2_ref.7, bf16[32,132608]{1,0:T(8,128)(2,1)} %h2_ref.7, bf16[32,132608]{1,0:T(8,128)(2,1)} %h2_ref.7, f32[4,512]{1,0:T(4,128)} %constant.12.clone.proto_ref, s32[1,32]{1,0:T(1,128)} %bitcast.11, ...), custom_call_target="tpu_custom_call" | custom-call | flops 3623878656 | bytes 9437184 | tf_op jit(solution)/shard_map/bank/pallas_call | solution.py:123
  29.5 5.9 %all-to-all-done.1.z_ref = bf16[16,32,1024]{2,1,0:T(8,128)(2,1)S(1)} async-done(((bf16[16,32,1024]{2,1,0:T(8,128)(2,1)}), bf16[16,32,1024]{2,1,0:T(8,128)(2,1)S(1)}, u32[]{:S(2)}, u32[]{:S(2)}) %all-to-all-start.1) | async-done | bytes 1048608 | tf_op jit(solution)/shard_map/all_to_all | solution.py:355
  35.4 6.8 %all-to-all-start = ((bf16[16,32,4608]{2,1,0:T(8,128)(2,1)}), bf16[16,32,4608]{2,1,0:T(8,128)(2,1)}, u32[]{:S(2)}, u32[]{:S(2)}) async-start(bf16[16,32,4608]{2,1,0:T(8,128)(2,1)} %bank.5), calls=%async_computation | async-start | bytes 9437184 | tf_op jit(solution)/shard_map/all_to_all | solution.py:355
  42.2 0.0 copy-start.1
  42.2 7.8 %bank.6 = bf16[16,32,1792]{2,1,0:T(8,128)(2,1)} custom-call(bf16[32,132608]{1,0:T(8,128)(2,1)} %h2_ref.7, bf16[32,132608]{1,0:T(8,128)(2,1)} %h2_ref.7, bf16[32,132608]{1,0:T(8,128)(2,1)} %h2_ref.7, bf16[32,132608]{1,0:T(8,128)(2,1)} %h2_ref.7, f32[4,512]{1,0:T(4,128)} %constant.12.clone.proto_ref, s32[1,32]{1,0:T(1,128)} %bitcast.12, ...), custom_call_target="tpu_custom_call" | custom-call | flops 1409286144 | bytes 3670016 | tf_op jit(solution)/shard_map/bank/pallas_call | solution.py:123
  50.0 0.0 copy-done.1
  50.0 5.9 %corr.4.past_ref = f32[32,2048]{1,0:T(8,128)S(1)} custom-call(bf16[16,32,1024]{2,1,0:T(8,128)(2,1)S(1)} %all-to-all-done.1.z_ref, s32[2,2048]{1,0:T(2,128)S(1)} %copy-done.1, f32[32,2048]{1,0:T(8,128)S(1)} %broadcast_in_dim.7.past_ref), custom_call_target="tpu_custom_call" | custom-call | flops 4294967296 | bytes 1048576 | tf_op jit(solution)/shard_map/corr/pallas_call | solution.py:191
  56.0 72.9 %all-to-all-done.z_ref = bf16[16,32,4608]{2,1,0:T(8,128)(2,1)} async-done(((bf16[16,32,4608]{2,1,0:T(8,128)(2,1)}), bf16[16,32,4608]{2,1,0:T(8,128)(2,1)}, u32[]{:S(2)}, u32[]{:S(2)}) %all-to-all-start) | async-done | bytes 4718624 | tf_op jit(solution)/shard_map/all_to_all | solution.py:355
  128.9 21.7 %all-to-all-start.3 = ((bf16[16,32,1792]{2,1,0:T(8,128)(2,1)}), bf16[16,32,1792]{2,1,0:T(8,128)(2,1)S(1)}, u32[]{:S(2)}, u32[]{:S(2)}) async-start(bf16[16,32,1792]{2,1,0:T(8,128)(2,1)} %bank.6), calls=%async_computation.3 | async-start | bytes 3670016 | tf_op jit(solution)/shard_map/all_to_all | solution.py:355
  150.7 4.4 %bank.4 = bf16[16,32,768]{2,1,0:T(8,128)(2,1)} custom-call(bf16[32,132608]{1,0:T(8,128)(2,1)} %h2_ref.7, bf16[32,132608]{1,0:T(8,128)(2,1)} %h2_ref.7, bf16[32,132608]{1,0:T(8,128)(2,1)} %h2_ref.7, bf16[32,132608]{1,0:T(8,128)(2,1)} %h2_ref.7, f32[4,512]{1,0:T(4,128)} %constant.12.clone.proto_ref, s32[1,32]{1,0:T(1,128)} %bitcast.13, ...), custom_call_target="tpu_custom_call" | custom-call | flops 603979776 | bytes 1572864 | tf_op jit(solution)/shard_map/bank/pallas_call | solution.py:123
  155.1 29.2 %corr.5.past_ref = f32[32,2048]{1,0:T(8,128)S(1)} custom-call(bf16[16,32,4608]{2,1,0:T(8,128)(2,1)} %all-to-all-done.z_ref, s32[2,2048]{1,0:T(2,128)S(1)} %copy-done.1, f32[32,2048]{1,0:T(8,128)S(1)} %corr.4.past_ref), custom_call_target="tpu_custom_call" | custom-call | flops 19327352832 | bytes 4718592 | tf_op jit(solution)/shard_map/corr/pallas_call | solution.py:191
  184.3 2.8 %all-to-all-done.3.z_ref = bf16[16,32,1792]{2,1,0:T(8,128)(2,1)S(1)} async-done(((bf16[16,32,1792]{2,1,0:T(8,128)(2,1)}), bf16[16,32,1792]{2,1,0:T(8,128)(2,1)S(1)}, u32[]{:S(2)}, u32[]{:S(2)}) %all-to-all-start.3) | async-done | bytes 1835040 | tf_op jit(solution)/shard_map/all_to_all | solution.py:355
  187.1 10.2 %all-to-all-start.2 = ((bf16[16,32,768]{2,1,0:T(8,128)(2,1)}), bf16[16,32,768]{2,1,0:T(8,128)(2,1)S(1)}, u32[]{:S(2)}, u32[]{:S(2)}) async-start(bf16[16,32,768]{2,1,0:T(8,128)(2,1)} %bank.4), calls=%async_computation.2 | async-start | bytes 1572864 | tf_op jit(solution)/shard_map/all_to_all | solution.py:355
  197.2 10.8 %corr.6.past_ref = f32[32,2048]{1,0:T(8,128)S(1)} custom-call(bf16[16,32,1792]{2,1,0:T(8,128)(2,1)S(1)} %all-to-all-done.3.z_ref, s32[2,2048]{1,0:T(2,128)S(1)} %copy-done.1, f32[32,2048]{1,0:T(8,128)S(1)} %corr.5.past_ref), custom_call_target="tpu_custom_call" | custom-call | flops 7516192768 | bytes 1835008 | tf_op jit(solution)/shard_map/corr/pallas_call | solution.py:191
  208.1 0.0 copy-start
  208.1 7.8 %all-to-all-done.2.z_ref = bf16[16,32,768]{2,1,0:T(8,128)(2,1)S(1)} async-done(((bf16[16,32,768]{2,1,0:T(8,128)(2,1)}), bf16[16,32,768]{2,1,0:T(8,128)(2,1)S(1)}, u32[]{:S(2)}, u32[]{:S(2)}) %all-to-all-start.2) | async-done | bytes 786464 | tf_op jit(solution)/shard_map/all_to_all | solution.py:355
  215.9 4.7 %corr.7 = f32[32,2048]{1,0:T(8,128)S(1)} custom-call(bf16[16,32,768]{2,1,0:T(8,128)(2,1)S(1)} %all-to-all-done.2.z_ref, s32[2,2048]{1,0:T(2,128)S(1)} %copy-done.1, f32[32,2048]{1,0:T(8,128)S(1)} %corr.6.past_ref), custom_call_target="tpu_custom_call" | custom-call | flops 3221225472 | bytes 786432 | tf_op jit(solution)/shard_map/corr/pallas_call | solution.py:191
  220.6 13.1 %all_to_all.25 = bf16[16,32,128]{2,1,0:T(8,128)(2,1)S(1)} all-to-all(bf16[16,32,128]{2,1,0:T(8,128)(2,1)S(1)} %bitcast_bitcast_fusion), channel_id=1, replica_groups=mesh['groups'=2,'wide'=16] {'wide'}, dimensions={0} | all-to-all | bytes 262144 | tf_op jit(solution)/shard_map/all_to_all | solution.py:361
  233.7 0.0 copy-done
  233.7 1.0 power.1
  (2 shorter events, 0.0 us)
Async XLA Ops:
  5.0 30.4 %all-to-all-start.1 = ((bf16[16,32,1024]{2,1,0:T(8,128)(2,1)}), bf16[16,32,1024]{2,1,0:T(8,128)(2,1)S(1)}, u32[]{:S(2)}, u32[]{:S(2)}) async-start(bf16[16,32,1024]{2,1,0:T(8,128)(2,1)} %bank.7), calls=%async_computation.1 | async-start | bytes 2097152 | tf_op jit(solution)/shard_map/all_to_all | solution.py:355
  35.4 93.5 %all-to-all-start = ((bf16[16,32,4608]{2,1,0:T(8,128)(2,1)}), bf16[16,32,4608]{2,1,0:T(8,128)(2,1)}, u32[]{:S(2)}, u32[]{:S(2)}) async-start(bf16[16,32,4608]{2,1,0:T(8,128)(2,1)} %bank.5), calls=%async_computation | async-start | bytes 9437184 | tf_op jit(solution)/shard_map/all_to_all | solution.py:355
  42.2 7.8 %copy-start.1 = (s32[2,2048]{1,0:T(2,128)S(1)}, s32[2,2048]{1,0:T(2,128)}, u32[]{:S(2)}) copy-start(s32[2,2048]{1,0:T(2,128)} %pairs_ref.7) | copy-start | bytes 49156
  128.9 58.2 %all-to-all-start.3 = ((bf16[16,32,1792]{2,1,0:T(8,128)(2,1)}), bf16[16,32,1792]{2,1,0:T(8,128)(2,1)S(1)}, u32[]{:S(2)}, u32[]{:S(2)}) async-start(bf16[16,32,1792]{2,1,0:T(8,128)(2,1)} %bank.6), calls=%async_computation.3 | async-start | bytes 3670016 | tf_op jit(solution)/shard_map/all_to_all | solution.py:355
  187.1 28.8 %all-to-all-start.2 = ((bf16[16,32,768]{2,1,0:T(8,128)(2,1)}), bf16[16,32,768]{2,1,0:T(8,128)(2,1)S(1)}, u32[]{:S(2)}, u32[]{:S(2)}) async-start(bf16[16,32,768]{2,1,0:T(8,128)(2,1)} %bank.4), calls=%async_computation.2 | async-start | bytes 1572864 | tf_op jit(solution)/shard_map/all_to_all | solution.py:355
  208.1 25.6 %copy-start = (bf16[512,512]{1,0:T(8,128)(2,1)S(1)}, bf16[512,512]{1,0:T(8,128)(2,1)}, u32[]{:S(2)}) copy-start(bf16[512,512]{1,0:T(8,128)(2,1)} %constant.15.clone.table_ref) | copy-start | bytes 1572868
